TPU v7x, 256 devices: a whole 4x4x8 slice. The times are simulated.
256 devices in a mesh: pairs: 64 (over y, z, core), orb: 4 (over x).
Axes of the slice: x: 4, y: 4, z: 8, core: 2. Of those that a mesh axis runs over, the one named last changes fastest.
Arguments:
- amplitudes: float32 [1024, 128, 128], P(('pairs', 'orb')), may hold values from -4 to 4
- integrals: bfloat16 [1024, 128, 128], P(('pairs', 'orb')), may hold values from -6 to 6
- energies: float32 [1024, 128], P(('pairs', 'orb')), may hold values from 0.5 to 4
- intersections: bfloat16 [1024, 16, 128, 128], P(('pairs', 'orb')), may hold values from -0.5 to 0.5
- couplings: float32 [1024, 16], P(('pairs', 'orb')), may hold values from -2 to 2
- projector: float32 [1024, 128], P(('pairs', 'orb')), may hold values from -0.5 to 0.5
- pair_orbitals: int32 [1024, 2], P(('pairs', 'orb')), may hold values from 0 to 31
- coupled: int32 [1024, 16], replicated, may hold values from 0 to 1023, as said below
- pair_slot: int32 [1024], replicated, may hold values from 0 to 1023, as said below
Outputs:
- final_amplitudes: float32 [1024, 128, 128], P(('pairs', 'orb'))
- residual: float32 [1024, 128, 128], P(('pairs', 'orb'))
Inputs may be any that keep to these rules, and one draw needn't show every extreme that they name: `coupled`: each row holds 16 different pair ids, never the id of the pair held in that row's slot. The rows of one device name at most 1 different pairs held by the devices of any one pairs index, and exactly 1 held by the devices of the next pairs index. `pair_slot`: A permutation of the pair ids.
All inputs are finite; a program needn't handle non-finite values.
Results may differ from a plain program's by a relative error of at most 0.00037.
Values may be sent and summed in bfloat16 or wider, within the bound.
A program may use at most 64 MiB of HBM per device.

v0:
```python
import jax
import jax.numpy as jnp
from jax import lax
from jax.sharding import PartitionSpec as P

PAIRS_ORB = 32
ITERS = 2


def body(
    amplitudes,
    integrals,
    energies,
    intersections,
    couplings,
    projector,
    pair_orbitals,
    coupled,
    pair_slot,
):
    highest = lax.Precision.HIGHEST
    pair_count = lax.axis_size("pairs")
    orb_count = lax.axis_size("orb")
    devices = pair_count * orb_count
    per_device = amplitudes.shape[0]
    width = amplitudes.shape[1]
    total = coupled.shape[0]
    capacity = 1 + coupled.shape[1] // pair_count
    group = orb_count * per_device
    orbitals = total // PAIRS_ORB
    pair_idx = lax.axis_index("pairs")
    orb_idx = lax.axis_index("orb")
    device_id = pair_idx * orb_count + orb_idx
    targets = pair_slot[coupled]
    row_owner = jnp.broadcast_to(
        (jnp.arange(total, dtype=jnp.int32) // per_device)[:, None], targets.shape
    )
    needed = jnp.zeros((devices, total), jnp.int32).at[row_owner, targets].set(1)
    mine = lax.dynamic_slice_in_dim(needed, device_id, 1, 0)[0].reshape(pair_count, group)
    ranks = (jnp.cumsum(mine, axis=1) - 1).reshape(total)
    own_targets = lax.dynamic_slice_in_dim(targets, device_id * per_device, per_device, 0)
    slot_ids = jnp.arange(capacity, dtype=jnp.int32)
    group_cols = lax.dynamic_slice_in_dim(needed, pair_idx * group, group, 1)
    group_rank = jnp.cumsum(group_cols, axis=1) - 1
    entry_pos = own_targets // group * capacity + ranks[own_targets]
    dest_cols = group_cols.reshape(pair_count, orb_count, group)
    dest_cols = lax.dynamic_slice_in_dim(dest_cols, orb_idx, 1, 1)[:, 0]
    dest_rank = group_rank.reshape(pair_count, orb_count, group)
    dest_rank = lax.dynamic_slice_in_dim(dest_rank, orb_idx, 1, 1)[:, 0]
    select = (
        (dest_cols == 1)[:, None, :] & (dest_rank[:, None, :] == slot_ids[None, :, None])
    ).astype(jnp.bfloat16)
    orbital_ids = jnp.arange(orbitals, dtype=jnp.int32)
    first_hot = (pair_orbitals[:, 0:1] == orbital_ids[None, :]).astype(jnp.float32)
    second_hot = (pair_orbitals[:, 1:2] == orbital_ids[None, :]).astype(jnp.float32)
    denom = energies[:, :, None] + energies[:, None, :]
    state = amplitudes
    residual = amplitudes
    for step in range(ITERS):
        blocks = state.astype(jnp.bfloat16)
        group_blocks = lax.all_gather(blocks, "orb", axis=0, tiled=True)
        outgoing = jnp.einsum(
            "pcj,jxy->pcxy", select, group_blocks, preferred_element_type=jnp.float32
        )
        outgoing = outgoing.astype(jnp.bfloat16)
        arrived = lax.all_to_all(outgoing, "pairs", split_axis=0, concat_axis=0, tiled=True)
        arrived = arrived.reshape(pair_count * capacity, width, width)
        fetched = arrived[entry_pos]
        lifted = jnp.einsum(
            "pkab,pkbc->pkac", intersections, fetched, preferred_element_type=jnp.float32
        )
        scaled = (couplings[:, :, None, None] * lifted).astype(jnp.bfloat16)
        coupling = jnp.einsum(
            "pkac,pkdc->pad", scaled, intersections, preferred_element_type=jnp.float32
        )
        projected = jnp.einsum("pab,pb->pa", state, projector, precision=highest)
        partial_sum = jnp.dot(first_hot.T, projected, precision=highest) + jnp.dot(
            second_hot.T, projected, precision=highest
        )
        summed = lax.psum(partial_sum, ("pairs", "orb"))
        left = jnp.dot(first_hot, summed, precision=highest)
        right = jnp.dot(second_hot, summed, precision=highest)
        residual = (
            integrals.astype(jnp.float32)
            + energies[:, :, None] * state
            + state * energies[:, None, :]
            - coupling
            + left[:, :, None] * projector[:, None, :]
            + projector[:, :, None] * right[:, None, :]
        )
        state = state - residual / denom
    return (state, residual)


def solution(mesh):
    return jax.shard_map(
        body,
        mesh=mesh,
        in_specs=(
            P(("pairs", "orb"), None, None),
            P(("pairs", "orb"), None, None),
            P(("pairs", "orb"), None),
            P(("pairs", "orb"), None, None, None),
            P(("pairs", "orb"), None),
            P(("pairs", "orb"), None),
            P(("pairs", "orb"), None),
            P(),
            P(),
        ),
        out_specs=(P(("pairs", "orb"), None, None), P(("pairs", "orb"), None, None)),
        check_vma=False,
    )
```

profile of v0, /device:TPU:1, one launch (start us, length us, event | category | flops | bytes accessed | tf_op | source)
XLA Modules:
  0.0 392.0 jit_solution(17940552267861765877)
XLA Ops:
  0.7 0.6 add_select_fusion
  1.9 0.8 compare_select_fusion.1
  3.1 65.3 %gather_fusion = s32[16384]{0:T(1024)S(1)} fusion(s32[1024]{0:T(1024)S(1)} %copy-done.1, s32[16384]{0:T(1024)S(1)} %broadcast_clamp_fusion), kind=kCustom, calls=%fused_computation | custom fusion | bytes 196608 | tf_op jit(solution)/shard_map/gather | solution.py:34
  69.8 0.6 broadcast.186
  70.4 60.8 %scatter_custom_fusion = s32[262144]{0:T(1024)S(1)} fusion(s32[16384]{0:T(1024)S(1)} %reshape.167, s32[16384]{0:T(1024)} %broadcast.186, s32[]{:T(128)} %constant.52.clone.1), kind=kCustom, calls=%fused_computation.28 | custom fusion | bytes 1049088
  131.2 1.1 reshape.134
  132.3 1.0 constant_dynamic-slice_fusion
  133.4 0.7 reduce_window_sum.22
  134.1 12.3 %all_gather.6 = bf16[16,128,128]{2,1,0:T(8,128)(2,1)S(1)} all-gather(bf16[4,128,128]{2,1,0:T(8,128)(2,1)S(1)} %convert_element_type.38), channel_id=1, replica_groups=mesh['pairs'=64,'orb'=4] {'orb'}, dimensions={0}, use_global_device_ids=true | all-gather | bytes 655360 | tf_op jit(solution)/shard_map/all_gather | solution.py:61
  146.4 0.7 convert_bitcast_fusion.1
  147.1 2.6 copy.45
  149.8 14.2 %all-to-all-start = ((bf16[64,1,128,128]{3,2,1,0:T(8,128)(2,1)}), bf16[64,1,128,128]{3,2,1,0:T(8,128)(2,1)}, u32[]{:S(2)}, u32[]{:S(2)}) async-start(bf16[64,1,128,128]{3,2,1,0:T(8,128)(2,1)} %copy.45), calls=%async_computation | async-start | bytes 4194304 | tf_op jit(solution)/shard_map/all_to_all | solution.py:66
  164.2 0.8 dynamic-slice_reduce_fusion
  165.4 0.7 gather_fusion.1
  167.4 89.2 %psum.14 = f32[32,128]{1,0:T(8,128)S(1)} all-reduce(f32[32,128]{1,0:T(8,128)S(1)} %convolution_add_fusion.1), channel_id=1, replica_groups=mesh['pairs'=64,'orb'=4] {'pairs','orb'}, use_global_device_ids=true, to_apply=%region_3.4 | all-reduce | flops 4096 | bytes 32768 | tf_op jit(solution)/shard_map/psum | solution.py:80
  257.1 3.7 gather_fusion.2
  260.8 3.8 fusion.64
  264.6 11.4 %all_gather.7 = bf16[16,128,128]{2,1,0:T(8,128)(2,1)S(1)} all-gather(bf16[4,128,128]{2,1,0:T(8,128)(2,1)S(1)} %get-tuple-element.4), channel_id=1, replica_groups=mesh['pairs'=64,'orb'=4] {'orb'}, dimensions={0}, use_global_device_ids=true | all-gather | bytes 655360 | tf_op jit(solution)/shard_map/all_gather | solution.py:61
  276.1 0.7 convert_bitcast_fusion
  276.8 2.6 copy.50
  279.4 11.7 %all-to-all-start.1 = ((bf16[64,1,128,128]{3,2,1,0:T(8,128)(2,1)}), bf16[64,1,128,128]{3,2,1,0:T(8,128)(2,1)}, u32[]{:S(2)}, u32[]{:S(2)}) async-start(bf16[64,1,128,128]{3,2,1,0:T(8,128)(2,1)} %copy.50), calls=%async_computation.1 | async-start | bytes 4194304 | tf_op jit(solution)/shard_map/all_to_all | solution.py:66
  292.2 91.1 %psum.15 = f32[32,128]{1,0:T(8,128)S(1)} all-reduce(f32[32,128]{1,0:T(8,128)S(1)} %convolution_add_fusion), channel_id=1, replica_groups=mesh['pairs'=64,'orb'=4] {'pairs','orb'}, use_global_device_ids=true, to_apply=%region_4.5 | all-reduce | flops 4096 | bytes 32768 | tf_op jit(solution)/shard_map/psum | solution.py:80
  383.7 3.7 gather_fusion.3
  387.4 4.6 %fusion.40 = (f32[4,128,128]{2,1,0:T(8,128)}, f32[4,128,128]{2,1,0:T(8,128)}) fusion(f32[4,128,128]{2,1,0:T(8,128)S(1)} %get-tuple-element.5, f32[4,128]{1,0:T(4,128)S(1)} %copy-done.12, f32[4,128]{1,0:T(4,128)S(1)} %fusion.49, f32[4,128]{1,0:T(4,128)S(1)} %copy-done.5, f32[4,128]{1,0:T(4,128)S(1)} %fusion.51, bf16[4,16,128,128]{3,2,1,0:T(8,128)(2,1)S(1)} %copy-done, ...), kind=kOutput, calls=%fused_computation.35 | convolution fusion | flops 539820032 | bytes 5120256 | tf_op jit(solution)/shard_map/pkac,pkdc->pad/dot_general | solution.py:73
  (67 shorter events, 6.0 us)
Async XLA Ops:
  0.6 260.2 %copy-start = (bf16[4,16,128,128]{3,2,1,0:T(8,128)(2,1)S(1)}, bf16[4,16,128,128]{3,2,1,0:T(8,128)(2,1)}, u32[]{:S(2)}) copy-start(bf16[4,16,128,128]{3,2,1,0:T(8,128)(2,1)} %param.12) | copy-start | bytes 6291460
  0.6 2.5 copy-start.1
  68.4 0.7 copy-start.3
  68.4 0.7 copy-start.4
  68.4 0.7 copy-start.6
  68.4 0.7 copy-start.9
  68.4 0.8 copy-start.8
  69.7 64.4 %copy-start.2 = (f32[4,128,128]{2,1,0:T(8,128)S(1)}, f32[4,128,128]{2,1,0:T(8,128)}, u32[]{:S(2)}) copy-start(f32[4,128,128]{2,1,0:T(8,128)} %param.9) | copy-start | bytes 786436
  149.8 107.3 %all-to-all-start = ((bf16[64,1,128,128]{3,2,1,0:T(8,128)(2,1)}), bf16[64,1,128,128]{3,2,1,0:T(8,128)(2,1)}, u32[]{:S(2)}, u32[]{:S(2)}) async-start(bf16[64,1,128,128]{3,2,1,0:T(8,128)(2,1)} %copy.45), calls=%async_computation | async-start | bytes 4194304 | tf_op jit(solution)/shard_map/all_to_all | solution.py:66
  164.0 2.4 copy-start.7
  164.0 2.4 copy-start.5
  257.0 3.8 copy-start.10
  257.0 3.8 copy-start.11
  257.1 3.8 copy-start.12
  279.4 104.3 %all-to-all-start.1 = ((bf16[64,1,128,128]{3,2,1,0:T(8,128)(2,1)}), bf16[64,1,128,128]{3,2,1,0:T(8,128)(2,1)}, u32[]{:S(2)}, u32[]{:S(2)}) async-start(bf16[64,1,128,128]{3,2,1,0:T(8,128)(2,1)} %copy.50), calls=%async_computation.1 | async-start | bytes 4194304 | tf_op jit(solution)/shard_map/all_to_all | solution.py:66
where the time goes:
time: 393 us; the launch traced here: 392 us
  blocking collectives  204 us (52%)
  local copies, waits for them, and re-layouts  145 us (37%)
  starting transfers between devices  25.9 us (7%)
  matrix products  12.6 us (3%)
    psum x2, blocking collectives, body(): summed = lax.psum(partial_sum, ('pairs', 'orb'))  180 us
    gather x3, local copies, waits for them, and re-layouts, body(): targets = pair_slot[coupled]  65.6 us
    unnamed x30, local copies, waits for them, and re-layouts  62.1 us
    all_to_all x2, starting transfers between devices, body(): lax.all_to_all(outgoing, 'pairs', split_axis=0, concat_axis=0, tiled=True)  25.9 us
    all_gather x2, blocking collectives, body(): group_blocks = lax.all_gather(blocks, 'orb', axis=0, tiled=True)  23.7 us
    dot_general x2, matrix products, body(): jnp.einsum('pkac,pkdc->pad', scaled, intersections, preferred_element_typ...  8.38 us
  transfers between devices with their start and end apart: 2, of which 0 were waited for; matrix products, arithmetic and copies ran while one was open for 1% of the time, Pallas kernels for 0%

commit v1 on v0

v1 whole, which is shorter than its diff:
```python
import functools

import jax
import jax.numpy as jnp
from jax import lax
from jax.experimental import pallas as pl
from jax.experimental.pallas import tpu as pltpu
from jax.sharding import PartitionSpec as P

ITERS = 2
NOCC = 32
NX, NY, NZ, NC = 4, 4, 8, 2
MESH = pl.DeviceIdType.MESH
HIGHEST = lax.Precision.HIGHEST
DESTS = [(dy, dc) for dy in range(NY) for dc in range(NC)]


def pair_index(y, z, c):
    return (y * NZ + z) * NC + c


def tables(coupled, pair_slot, per_device):
    pair_idx = lax.axis_index("pairs")
    x = lax.axis_index("orb")
    y, z, c = pair_idx // (NZ * NC), pair_idx // NC % NZ, pair_idx % NC
    total = pair_slot.shape[0]
    group = NX * per_device
    back = jnp.arange(NZ, dtype=jnp.int32)
    source = pair_index(y, (z - back) % NZ, c)
    slots = source[:, None] * group + jnp.arange(group, dtype=jnp.int32)[None, :]
    ids = jnp.arange(total, dtype=jnp.int32)
    held = jnp.sum(
        jnp.where(pair_slot[None, None, :] == slots[:, :, None], ids[None, None, :], 0), axis=2
    )
    dy = jnp.arange(NY * NC, dtype=jnp.int32) // NC
    dc = jnp.arange(NY * NC, dtype=jnp.int32) % NC
    receiver = pair_index((y + dy) % NY, z, (c + dc) % NC) * NX + x
    rows = (receiver[:, None] * per_device + jnp.arange(per_device, dtype=jnp.int32)[None, :]).reshape(-1)
    wanted = coupled[rows].reshape(NY * NC, -1)
    place = jnp.arange(group, dtype=jnp.int32)
    place = (place // per_device - x) % NX * per_device + place % per_device
    select = jnp.max(
        jnp.where(
            held[:, None, :, None] == wanted[None, :, None, :], place[None, None, :, None], 0
        ),
        axis=(2, 3),
    )
    target = pair_slot[wanted[0]] // group
    ty, tz, tc = target // (NZ * NC), target // NC % NZ, target % NC
    entry = (((y - ty) % NY) * NC + (c + tc) % NC) * NZ + (z - tz) % NZ
    return select.reshape(-1), entry


def kernel(
    select, entry, orbs, coup, amp, integ_hbm, ener, inter_hbm, proj, fin, res,
    *scratch,
):
    gath = [scratch[0:NZ], scratch[NZ : 2 * NZ]]
    out_buf = scratch[2 * NZ : 2 * NZ + 2]
    recv = scratch[2 * NZ + 2 : 2 * NZ + 4]
    (parts, part_y, part_x, part_z, inter, integ, state, den, pcol, base, local_sem, blk_send, blk_recv,
     y_send, y_recv, p_send, p_recv) = scratch[2 * NZ + 4 :]
    per = amp.shape[0]
    width = amp.shape[1]
    nb = inter.shape[0] // per
    pair_idx = lax.axis_index("pairs")
    x = lax.axis_index("orb")
    y, z, c = pair_idx // (NZ * NC), lax.rem(pair_idx // NC, NZ), lax.rem(pair_idx, NC)

    def dev(dx=0, dy=0, dz=0, dc=0):
        return (
            pair_index(lax.rem(y + dy, NY), lax.rem(z + dz, NZ), lax.rem(c + dc, NC)),
            lax.rem(x + dx, NX),
        )

    inter_copy = pltpu.make_async_copy(inter_hbm, inter, local_sem.at[0])
    integ_copy = pltpu.make_async_copy(integ_hbm, integ, local_sem.at[1])
    inter_copy.start()
    integ_copy.start()

    peers = [dev(dx=d) for d in range(1, NX)]
    peers += [dev(dy=dy, dc=dc) for dy, dc in DESTS[1:]]
    peers += [dev(dz=d) for d in range(1, NZ)]
    barrier = pltpu.get_barrier_semaphore()
    for peer in peers:
        pl.semaphore_signal(barrier, inc=1, device_id=peer, device_id_type=MESH)

    for s in range(per):
        state[s] = amp[s]
        gath[0][0][s] = amp[s].astype(jnp.bfloat16)
    pl.semaphore_wait(barrier, len(peers))

    sent = []

    def send(src, dst, ssem, rsem, to):
        copy = pltpu.make_async_remote_copy(
            src_ref=src, dst_ref=dst, send_sem=ssem, recv_sem=rsem, device_id=to, device_id_type=MESH
        )
        copy.start()
        sent.append(copy)

    def arrived(ref, sem):
        pltpu.make_async_copy(ref, ref, sem).wait()

    def column(row):
        return jnp.broadcast_to(row, (width, width)).T

    for it in range(ITERS):
        g = gath[it]
        sems = blk_recv.at[it]

        def part(k, q, g=g):
            return g[k].at[pl.ds(q * per, per)]

        def push(k, q, k2, q2, to, sems=sems, part=part, it=it):
            send(part(k, q), part(k2, q2), blk_send.at[it], sems.at[q2 * NZ + k2], to)

        def ready(k, q, sems=sems, part=part):
            arrived(part(k, q), sems.at[q * NZ + k])

        def deliver(k, it=it, g=g, ready=ready):
            ready(k, 2)
            ready(k, 3)
            for i, (dy, dc) in enumerate(DESTS):
                block = g[k][select[k * len(DESTS) + i]]
                if i == 0:
                    recv[it][k] = block
                else:
                    out_buf[it][k * (len(DESTS) - 1) + i - 1] = block
            for i, (dy, dc) in enumerate(DESTS):
                if i:
                    send(
                        out_buf[it].at[k * (len(DESTS) - 1) + i - 1],
                        recv[it].at[i * NZ + k],
                        y_send.at[it],
                        y_recv.at[it],
                        dev(dy=dy, dc=dc),
                    )

        up, down, right, left = dev(dz=1), dev(dz=NZ - 1), dev(dx=1), dev(dx=NX - 1)
        push(0, 0, 1, 0, up)
        push(0, 0, 7, 0, down)
        push(0, 0, 0, 1, left)
        push(0, 0, 0, 3, right)

        orbital = lax.broadcasted_iota(jnp.int32, (NOCC, width), 0)
        total = jnp.zeros((NOCC, width), jnp.float32)
        for s in range(per):
            row = lax.dot_general(
                jnp.broadcast_to(proj[s : s + 1, :], (8, width)),
                state[s],
                (((1,), (1,)), ((), ())),
                precision=HIGHEST,
                preferred_element_type=jnp.float32,
            )[0:1]
            row = jnp.broadcast_to(row, (NOCC, width))
            total += jnp.where(orbital == orbs[2 * s], row, 0.0)
            total += jnp.where(orbital == orbs[2 * s + 1], row, 0.0)
        p = parts.at[it]
        p[0] = total
        for i, (dy, dc) in enumerate(DESTS):
            if i:
                send(p.at[0], part_y.at[it, i - 1], p_send.at[it], p_recv.at[it, 0], dev(dy=dy, dc=dc))

        ready(0, 1)
        push(0, 1, 1, 1, up)
        push(0, 1, 7, 1, down)
        push(0, 1, 0, 2, left)

        if it == 0:
            integ_copy.wait()
            for s in range(per):
                e_row = ener[s : s + 1, :]
                den[s] = column(e_row) + e_row
                pcol[s] = column(proj[s : s + 1, :])
        for s in range(per):
            base[s] = integ[s].astype(jnp.float32) + den[s] * state[s]

        for q, (f, to) in enumerate(((3, right), (2, left))):
            ready(1, q)
            push(1, q, 2, q, up)
            ready(7, q)
            push(7, q, 6, q, down)
            push(1, q, 1, f, to)
            push(7, q, 7, f, to)

        arrived(part_y.at[it], p_recv.at[it, 0])
        total = p[0]
        for i in range(len(DESTS) - 1):
            total += part_y[it, i]
        p[1] = total
        for d in range(1, NX):
            send(p.at[1], part_x.at[it, d - 1], p_send.at[it], p_recv.at[it, 1], dev(dx=d))

        deliver(0)
        for q, (f, to) in enumerate(((3, right), (2, left))):
            ready(2, q)
            push(2, q, 3, q, up)
            ready(6, q)
            push(6, q, 5, q, down)
            push(2, q, 2, f, to)
            push(6, q, 6, f, to)
        deliver(1)
        deliver(7)

        arrived(part_x.at[it], p_recv.at[it, 1])
        total = p[1]
        for i in range(NX - 1):
            total += part_x[it, i]
        p[2] = total
        for d in range(1, NZ):
            send(p.at[2], part_z.at[it, d - 1], p_send.at[it], p_recv.at[it, 2], dev(dz=d))

        for q, (f, to) in enumerate(((3, right), (2, left))):
            ready(3, q)
            ready(5, q)
            if q == 0:
                push(3, q, 4, q, up)
            else:
                push(5, q, 4, q, down)
            push(3, q, 3, f, to)
            push(5, q, 5, f, to)
        deliver(2)
        deliver(6)
        ready(4, 0)
        push(4, 0, 4, 3, right)
        ready(4, 1)
        push(4, 1, 4, 2, left)
        deliver(3)
        deliver(5)
        deliver(4)

        arrived(part_z.at[it], p_recv.at[it, 2])
        total = p[2]
        for i in range(NZ - 1):
            total += part_z[it, i]
        p[3] = total

        if it == 0:
            inter_copy.wait()
        arrived(recv[it].at[pl.ds(NZ, (len(DESTS) - 1) * NZ)], y_recv.at[it])

        def one_slot(s, carry, it=it, p=p):
            acc = jnp.zeros((width, width), jnp.float32)
            for k in range(nb):
                own = inter[s * nb + k]
                lifted = jnp.dot(own, recv[it][entry[s * nb + k]], preferred_element_type=jnp.float32)
                scaled = (coup[s * nb + k] * lifted).astype(jnp.bfloat16)
                acc += lax.dot_general(
                    scaled, own, (((1,), (1,)), ((), ())), preferred_element_type=jnp.float32
                )
            left_row = p[3, pl.ds(orbs[2 * s], 1), :]
            right_row = p[3, pl.ds(orbs[2 * s + 1], 1), :]
            resid = (
                base[s] - acc + column(left_row) * proj[pl.ds(s, 1), :] + pcol[s] * right_row
            )
            new = state[s] - resid / den[s]
            if it == ITERS - 1:
                res[s] = resid
                fin[s] = new
            else:
                state[s] = new
                gath[it + 1][0][s] = new.astype(jnp.bfloat16)
            return carry

        lax.fori_loop(0, per, one_slot, 0)

    for copy in sent:
        copy.wait_send()


def body(amplitudes, integrals, energies, intersections, couplings, projector, pair_orbitals, coupled, pair_slot):
    per, width, _ = amplitudes.shape
    nb = coupled.shape[1]
    group = NX * per
    receivers = len(DESTS)
    select, entry = tables(coupled, pair_slot, per)
    bf16, f32 = jnp.bfloat16, jnp.float32
    vmem = pl.BlockSpec(memory_space=pltpu.VMEM)
    smem = pl.BlockSpec(memory_space=pltpu.SMEM)
    hbm = pl.BlockSpec(memory_space=pl.ANY)
    dma = pltpu.SemaphoreType.DMA
    square = (per, width, width)
    scratch = [pltpu.VMEM((group, width, width), bf16) for _ in range(2 * NZ)]
    scratch += [pltpu.VMEM((NZ * (receivers - 1), width, width), bf16) for _ in range(2)]
    scratch += [pltpu.VMEM((NZ * receivers, width, width), bf16) for _ in range(2)]
    scratch += [
        pltpu.VMEM((ITERS, 4, NOCC, width), f32),
        pltpu.VMEM((ITERS, receivers - 1, NOCC, width), f32),
        pltpu.VMEM((ITERS, NX - 1, NOCC, width), f32),
        pltpu.VMEM((ITERS, NZ - 1, NOCC, width), f32),
        pltpu.VMEM((per * nb, width, width), bf16),
        pltpu.VMEM(square, bf16),
        pltpu.VMEM(square, f32),
        pltpu.VMEM(square, f32),
        pltpu.VMEM(square, f32),
        pltpu.VMEM(square, f32),
        dma((2,)),
        dma((ITERS,)),
        dma((ITERS, 4 * NZ)),
        dma((ITERS,)),
        dma((ITERS,)),
        dma((ITERS,)),
        dma((ITERS, 3)),
    ]
    return pl.pallas_call(
        kernel,
        out_shape=(
            jax.ShapeDtypeStruct(square, f32),
            jax.ShapeDtypeStruct(square, f32),
        ),
        in_specs=[smem, smem, smem, smem, vmem, hbm, vmem, hbm, vmem],
        out_specs=(vmem, vmem),
        scratch_shapes=scratch,
        compiler_params=pltpu.CompilerParams(
            collective_id=0, has_side_effects=True, vmem_limit_bytes=48 * 1024 * 1024
        ),
    )(
        select,
        entry,
        pair_orbitals.reshape(-1),
        couplings.reshape(-1),
        amplitudes,
        integrals,
        energies,
        intersections.reshape(per * nb, width, width),
        projector,
    )


def solution(mesh):
    both = ("pairs", "orb")
    return jax.shard_map(
        body,
        mesh=mesh,
        in_specs=(
            P(both, None, None),
            P(both, None, None),
            P(both, None),
            P(both, None, None, None),
            P(both, None),
            P(both, None),
            P(both, None),
            P(),
            P(),
        ),
        out_specs=(P(both, None, None), P(both, None, None)),
        check_vma=False,
    )
```

time: 393 us -> 111 us (0.28)
  blocking collectives: 204 us -> 0 us
  local copies, waits for them, and re-layouts: 145 us -> 11.2 us
  Pallas kernels: 0 us -> 96.3 us
  starting transfers between devices: 25.9 us -> 0 us
  matrix products: 12.6 us -> 0 us
    psum x2 -> x0, blocking collectives: 180 us -> none  [body(): summed = lax.psum(partial_sum, ('pairs', 'orb'))]
    pallas_call x0 -> x1, Pallas kernels: none -> 96.3 us  [body(): pl.pallas_call(kernel, out_shape=(jax.ShapeDtypeStruct(square, f32), jax....]
    gather x7 -> x2, local copies, waits for them, and re-layouts: 73.9 us -> 2.04 us  [the longest x1 1.47 us: tables(): target = pair_slot[wanted[0]] // group]
    unnamed x30 -> x14, local copies, waits for them, and re-layouts: 62.1 us -> 8.01 us
    all_to_all x2 -> x0, starting transfers between devices: 25.9 us -> none  [body(): lax.all_to_all(outgoing, 'pairs', split_axis=0, concat_axis=0, tiled=True)]
    all_gather x2 -> x0, blocking collectives: 23.7 us -> none  [body(): group_blocks = lax.all_gather(blocks, 'orb', axis=0, tiled=True)]
    dot_general x14 -> x0, matrix products: 12.6 us -> none  [the longest x2 8.38 us: body(): jnp.einsum('pkac,pkdc->pad', scaled, intersections, preferred_element_typ...]
    convert_element_type x2 -> x0, local copies, waits for them, and re-layouts: 5.29 us -> none  [body(): outgoing = outgoing.astype(jnp.bfloat16)]
  transfers between devices with their start and end apart: 2 -> 0, of which waited for: 0 -> 0; matrix products, arithmetic and copies ran while one was open for 1% -> 0% of each run, Pallas kernels for 0% -> 0%
where the time goes in v1:
time: 111 us
  Pallas kernels  96.3 us (87%)
  local copies, waits for them, and re-layouts  11.2 us (10%)
  other arithmetic  2.61 us (2%)
    pallas_call x1, Pallas kernels, body(): pl.pallas_call(kernel, out_shape=(jax.ShapeDtypeStruct(square, f32), jax....  96.3 us
    unnamed x14, local copies, waits for them, and re-layouts  8.01 us

profile of v1, /device:TPU:1, one launch (start us, length us, event | category | flops | bytes accessed | tf_op | source)
XLA Modules:
  0.0 110.9 jit_solution(2150770268975767246)
XLA Ops:
  0.7 0.8 reshape.210.coup
  1.5 0.8 copy.16
  2.2 0.1 reshape.209.orbs
  2.3 0.1 iota_add_fusion.1
  2.4 1.0 select_reduce_fusion.1
  3.4 0.1 iota_add_fusion
  3.5 0.1 add.268
  3.6 1.0 copy.15
  4.6 0.6 gather_fusion
  5.2 0.1 eq.49
  5.3 1.4 %select_reduce_fusion = s32[8,8]{1,0:T(8,128)S(1)} fusion(s32[16]{0:T(128)S(1)} %fusion, s32[8,64]{1,0:T(8,128)S(1)} %eq.49, s32[8,16]{1,0:T(8,128)S(1)} %select_reduce_fusion.1), kind=kLoop, calls=%fused_computation.2 | loop fusion | flops 196544 | bytes 2880 | tf_op jit(solution)/shard_map/reduce_max | solution.py:42
  6.6 0.1 reshape.208.select
  6.7 0.1 squeeze.3
  6.8 1.5 %gather_fusion.1 = s32[64]{0:T(128)S(1)} fusion(s32[1024]{0:T(1024)} %param.17, s32[1024]{0:T(1024)S(1)} %pad_clamp_fusion), kind=kCustom, calls=%fused_computation.1 | custom fusion | bytes 768 | tf_op jit(solution)/shard_map/gather | solution.py:48
  8.3 0.0 copy-start
  8.3 1.6 %copy-done = bf16[4,16,128,128]{3,2,1,0:T(8,128)(2,1)S(1)} copy-done((bf16[4,16,128,128]{3,2,1,0:T(8,128)(2,1)S(1)}, bf16[4,16,128,128]{3,2,1,0:T(8,128)(2,1)}, u32[]{:S(2)}) %copy-start) | copy-done | bytes 2097176
  9.9 0.0 copy-start.1
  9.9 0.9 copy-done.1
  10.9 0.9 copy-done.2
  11.8 0.7 copy-done.3
  12.5 0.7 copy-done.4
  13.1 96.3 %shard_map.104 = (f32[4,128,128]{2,1,0:T(8,128)S(1)}, f32[4,128,128]{2,1,0:T(8,128)S(1)}) custom-call(s32[64]{0:T(128)S(1)} %reshape.208.select, s32[64]{0:T(128)S(1)} %fusion.4.entry, s32[8]{0:T(128)S(1)} %reshape.209.orbs, f32[64]{0:T(128)S(1)} %reshape.210.coup, f32[4,128,128]{2,1,0:T(8,128)S(1)} %copy-done.1, bf16[4,128,128]{2,1,0:T(8,128)(2,1)S(1)} %copy-done.2, ...), custom_call_target="tpu_custom_call" | custom-call | tf_op jit(solution)/shard_map/pallas_call | solution.py:306
  109.5 0.7 copy.19
  110.2 0.7 copy.20
  (11 shorter events, 0.1 us)
Async XLA Ops:
  8.3 1.6 %copy-start = (bf16[4,16,128,128]{3,2,1,0:T(8,128)(2,1)S(1)}, bf16[4,16,128,128]{3,2,1,0:T(8,128)(2,1)}, u32[]{:S(2)}) copy-start(bf16[4,16,128,128]{3,2,1,0:T(8,128)(2,1)} %param.12) | copy-start | bytes 6291460
  9.9 0.9 copy-start.1
  10.9 0.9 copy-start.2
  11.8 0.7 copy-start.3
  12.5 0.7 copy-start.4

commit v2 on v1

v2 whole, which is shorter than its diff:
```python
import jax
import jax.numpy as jnp
from jax import lax
from jax.experimental import pallas as pl
from jax.experimental.pallas import tpu as pltpu
from jax.sharding import PartitionSpec as P

ITERS = 2
NOCC = 32
NX, NY, NZ, NC = 4, 4, 8, 2
PLANE = NX * NY * NC
MESH = pl.DeviceIdType.MESH
HIGHEST = lax.Precision.HIGHEST
ROUNDS = ((0,), (1, 7), (2, 6), (3, 5), (4,))
FIRST = {0: 0, 1: 1, 2: 3, 3: 5, 4: 7}


def pair_index(y, z, c):
    return (y * NZ + z) * NC + c


def kernel(
    coup, orbs, slot_of, amp_hbm, integ_hbm, ener_hbm, inter_hbm, proj_hbm, coupled_hbm, slots_hbm, fin, res,
    *scratch,
):
    gath = [scratch[0:NZ], scratch[NZ : 2 * NZ]]
    out_buf = scratch[2 * NZ : 2 * NZ + 2]
    recv = scratch[2 * NZ + 2 : 2 * NZ + 4]
    blocks = scratch[2 * NZ + 4 : 2 * NZ + 6]
    (parts, full, half, part_y, part_x, part_z, sums, inter, integ, state, ener, proj, cpl, slots, den, pcol, base,
     sel_v, want_v, sel, want, entry,
     local_sem, x_send, x_recv, z_send, z_recv, y_send, y_recv, p_send, p_recv) = scratch[2 * NZ + 6 :]
    per, width, _ = state.shape
    nb = inter.shape[0] // per
    group = NX * per
    quarter = width // NX
    pair_idx = lax.axis_index("pairs")
    x = lax.axis_index("orb")
    y, z, c = pair_idx // (NZ * NC), pair_idx // NC % NZ, pair_idx % NC

    xs = [(x + d) % NX for d in range(NX)]
    ys = [(y + d) % NY for d in range(NY)]
    zs = [(z + d) % NZ for d in range(NZ)]
    cs = [(c + d) % NC for d in range(NC)]

    def dev(dx=0, dy=0, dz=0, dc=0):
        return (pair_index(ys[dy], zs[dz], cs[dc]), xs[dx])

    steps = [(dx, dy, dc) for dx in range(NX) for dy in range(NY) for dc in range(NC)]

    local = [
        pltpu.make_async_copy(a, b, local_sem.at[i])
        for i, (a, b) in enumerate(
            (
                (amp_hbm, state),
                (coupled_hbm, cpl),
                (slots_hbm, slots),
                (proj_hbm, proj),
                (ener_hbm, ener),
                (integ_hbm, integ),
                (inter_hbm, inter),
            )
        )
    ]
    for copy in local:
        copy.start()

    barrier = pltpu.get_barrier_semaphore()

    for d in range(1, NZ):
        pl.semaphore_signal(barrier, inc=1, device_id=dev(dz=d), device_id_type=MESH)
    for dx, dy, dc in steps[1:]:
        pl.semaphore_signal(barrier, inc=1, device_id=dev(dx, dy, 0, dc), device_id_type=MESH)

    local[0].wait()
    for s in range(per):
        blocks[0][s] = state[s].astype(jnp.bfloat16)

    sent = []

    def send(src, dst, ssem, rsem, to):
        copy = pltpu.make_async_remote_copy(
            src_ref=src, dst_ref=dst, send_sem=ssem, recv_sem=rsem, device_id=to, device_id_type=MESH
        )
        copy.start()
        return copy

    def arrived(ref, sem):
        pltpu.make_async_copy(ref, ref, sem).wait()

    def column(row):
        return jnp.broadcast_to(row, (width, width)).T

    def make_tables():
        local[1].wait()
        local[2].wait()
        lane = lax.broadcasted_iota(jnp.int32, (nb, width), 1)
        span = width // NY
        wanted = jnp.zeros((nb, width), jnp.int32)
        for yy in range(NY):
            start = pl.multiple_of(yy * (NZ * span) + z // NY * width, width)
            tile = cpl[:, pl.ds(start, width)]
            tile = pltpu.roll(tile, (yy * span + width - z % NY * span) % width, 1)
            wanted = jnp.where(lane // span == yy, tile, wanted)
        want_v[...] = wanted
        row = lax.broadcasted_iota(jnp.int32, (width, width), 0)
        col = lax.broadcasted_iota(jnp.int32, (width, width), 1)
        slot = pair_index(y, (z + NZ - row // group) % NZ, c) * group + row % group
        held = jnp.zeros((width, width), jnp.int32)
        for r in range(slots.shape[0]):
            held += jnp.where(slots[r : r + 1, :] == slot, col + r * width, 0)
        shift = width // 2
        while shift:
            held += pltpu.roll(held, shift, 1)
            shift //= 2
        hits = jnp.zeros((width, width), jnp.int32)
        for e in range(nb):
            hits = jnp.maximum(hits, jnp.where(wanted[e : e + 1, :] == held, row % group, 0))
        best = hits
        for r in range(1, per):
            best = jnp.maximum(best, pltpu.roll(hits, width - r, 1))
        sel_v[...] = jnp.max(best.reshape(NZ, group, width), axis=1)
        a = pltpu.make_async_copy(sel_v, sel, local_sem.at[len(local)])
        b = pltpu.make_async_copy(want_v, want, local_sem.at[len(local) + 1])
        a.start()
        b.start()
        a.wait()
        b.wait()

    def make_entries():
        mine = ((y * NC + c) * NX + x) * per

        def one(i, carry):
            t = slot_of[want[i % nb, mine + i // nb]] // group
            ty, tz, tc = t // (NZ * NC), t // NC % NZ, t % NC
            k = (z - tz + NZ) % NZ
            order = jnp.where(k <= NZ // 2, jnp.maximum(2 * k - 1, 0), 2 * (NZ - k))
            entry[i] = ((y - ty + NY) % NY * NC + (c + tc) % NC) * NZ + order
            return carry

        lax.fori_loop(0, per * nb, one, 0)

    own_rows = pl.ds(pl.multiple_of(x * quarter, quarter), quarter)

    def spread(it, s):
        for d in range(1, NX):
            theirs = pl.ds(pl.multiple_of(xs[d] * quarter, quarter), quarter)
            send(
                blocks[it].at[s, theirs],
                gath[it][0].at[x * per + s],
                x_send.at[it],
                x_recv.at[it],
                dev(dx=d),
            )
        gath[it][0][x * per + s] = blocks[it][s, own_rows, :]

    def singles_terms(it):
        if it == 0:
            local[3].wait()
        orbital = lax.broadcasted_iota(jnp.int32, (NOCC, width), 0)
        total = jnp.zeros((NOCC, width), jnp.float32)
        for s in range(per):
            row = lax.dot_general(
                jnp.broadcast_to(proj[s : s + 1, :], (8, width)),
                state[s],
                (((1,), (1,)), ((), ())),
                precision=HIGHEST,
                preferred_element_type=jnp.float32,
            )[0:1]
            row = jnp.broadcast_to(row, (NOCC, width))
            total += jnp.where(orbital == orbs[s, 0], row, 0.0)
            total += jnp.where(orbital == orbs[s, 1], row, 0.0)
        parts[it] = total

    for it in range(ITERS):
        g = gath[it]

        def push(k, h, k2, to, g=g, it=it):
            def part(j):
                return g[j].at[pl.ds(h * (group // 2), group // 2)]

            sent.append(send(part(k), part(k2), z_send.at[it], z_recv.at[it, k2 * 2 + h], to))

        def ready(k, h, g=g, it=it):
            arrived(g[k].at[pl.ds(h * (group // 2), group // 2)], z_recv.at[it, k * 2 + h])

        def deliver(ks, it=it, g=g):
            first, count = FIRST[ks[0]], len(ks)

            for i, (dx, dy, dc) in enumerate(steps):
                at = ((ys[dy] * NC + cs[dc]) * NX + xs[dx]) * per
                for j, k in enumerate(ks):
                    out_buf[it][i, first + j] = g[k][sel[k, at]]
            for j in range(count):
                recv[it][first + j, own_rows, :] = out_buf[it][0, first + j]
            for i, (dx, dy, dc) in enumerate(steps):
                if i:
                    send(
                        out_buf[it].at[i, pl.ds(first, count)],
                        recv[it].at[pl.ds((dy * NC + dc) * NZ + first, count), own_rows],
                        y_send.at[it],
                        y_recv.at[it],
                        dev(dx, dy, 0, dc),
                    )

        if it == 0:
            singles_terms(0)
            make_tables()
            pl.semaphore_wait(barrier, PLANE - 1 + NZ - 1)
            for s in range(per):
                spread(0, s)
        else:
            singles_terms(it)
        share = NOCC // NC
        mine = pl.ds(pl.multiple_of(c * share, share), share)
        other = pl.ds(pl.multiple_of((1 - c) * share, share), share)
        sent.append(send(parts.at[it, other], half.at[it], p_send.at[it, 0], p_recv.at[it, 0], dev(dc=1)))

        up, down = dev(dz=1), dev(dz=NZ - 1)
        arrived(g[0].at[pl.ds(0, group - per)], x_recv.at[it])
        for h in range(2):
            push(0, h, 1, up)
            push(0, h, 7, down)
        deliver((0,))

        arrived(half.at[it], p_recv.at[it, 0])
        sums[it, 0] = parts[it, mine, :] + half[it]
        for d in range(1, NY):
            sent.append(send(sums.at[it, 0], part_y.at[it, d - 1], p_send.at[it, 1], p_recv.at[it, 1], dev(dy=d)))

        for h in range(2):
            ready(1, h)
            push(1, h, 2, up)
            ready(7, h)
            push(7, h, 6, down)
        deliver((1, 7))

        arrived(part_y.at[it], p_recv.at[it, 1])
        sums[it, 1] = sums[it, 0] + part_y[it, 0] + part_y[it, 1] + part_y[it, 2]
        for d in range(1, NX):
            sent.append(send(sums.at[it, 1], part_x.at[it, d - 1], p_send.at[it, 2], p_recv.at[it, 2], dev(dx=d)))

        for h in range(2):
            ready(2, h)
            push(2, h, 3, up)
            ready(6, h)
            push(6, h, 5, down)
        deliver((2, 6))

        arrived(part_x.at[it], p_recv.at[it, 2])
        sums[it, 2] = sums[it, 1] + part_x[it, 0] + part_x[it, 1] + part_x[it, 2]
        for d in range(1, NZ):
            sent.append(send(sums.at[it, 2], part_z.at[it, d - 1], p_send.at[it, 3], p_recv.at[it, 3], dev(dz=d)))

        ready(3, 0)
        push(3, 0, 4, up)
        ready(5, 1)
        push(5, 1, 4, down)
        ready(5, 0)
        ready(3, 1)
        deliver((3, 5))
        ready(4, 0)
        ready(4, 1)
        deliver((4,))

        arrived(part_z.at[it], p_recv.at[it, 3])
        total = sums[it, 2]
        for i in range(NZ - 1):
            total += part_z[it, i]
        full[it, mine, :] = total
        sums[it, 3] = total
        sent.append(send(sums.at[it, 3], half.at[ITERS + it], p_send.at[it, 4], p_recv.at[it, 4], dev(dc=1)))

        if it == 0:
            make_entries()
            local[4].wait()
            local[5].wait()
            for s in range(per):
                e_row = ener[s : s + 1, :]
                den[s] = column(e_row) + e_row
                pcol[s] = column(proj[s : s + 1, :])
        for s in range(per):
            base[s] = integ[s].astype(jnp.float32) + den[s] * state[s]

        arrived(half.at[ITERS + it], p_recv.at[it, 4])
        full[it, other, :] = half[ITERS + it]
        if it == 0:
            local[6].wait()
        arrived(recv[it].at[pl.ds(0, (PLANE - 1) * NZ // NX)], y_recv.at[it])

        def one_slot(s, carry, it=it):
            acc = jnp.zeros((width, width), jnp.float32)
            for k in range(nb):
                own = inter[s * nb + k]
                lifted = jnp.dot(own, recv[it][entry[s * nb + k]], preferred_element_type=jnp.float32)
                scaled = (coup[s, k] * lifted).astype(jnp.bfloat16)
                acc += lax.dot_general(
                    scaled, own, (((1,), (1,)), ((), ())), preferred_element_type=jnp.float32
                )
            left_row = full[it, pl.ds(orbs[s, 0], 1), :]
            right_row = full[it, pl.ds(orbs[s, 1], 1), :]
            resid = base[s] - acc + column(left_row) * proj[pl.ds(s, 1), :] + pcol[s] * right_row
            new = state[s] - resid / den[s]
            if it == ITERS - 1:
                res[s] = resid
                fin[s] = new
            else:
                state[s] = new
                blocks[it + 1][s] = new.astype(jnp.bfloat16)
                spread(it + 1, s)
            return carry

        lax.fori_loop(0, per, one_slot, 0)

    for copy in sent:
        copy.wait_send()
    for it in range(ITERS):
        arrived(gath[it][0].at[pl.ds(0, group - per)], x_send.at[it])
        sends = recv[it].at[pl.ds(0, (PLANE - 1) * NZ // NX)]
        arrived(sends, y_send.at[it])


def body(amplitudes, integrals, energies, intersections, couplings, projector, pair_orbitals, coupled, pair_slot):
    per, width, _ = amplitudes.shape
    nb = coupled.shape[1]
    total = pair_slot.shape[0]
    group = NX * per
    quarter = width // NX
    bf16, f32, i32 = jnp.bfloat16, jnp.float32, jnp.int32
    vmem = pl.BlockSpec(memory_space=pltpu.VMEM)
    smem = pl.BlockSpec(memory_space=pltpu.SMEM)
    hbm = pl.BlockSpec(memory_space=pltpu.HBM)
    dma = pltpu.SemaphoreType.DMA
    square = (per, width, width)
    share = NOCC // NC
    scratch = [pltpu.VMEM((group, quarter, width), bf16) for _ in range(2 * NZ)]
    scratch += [pltpu.VMEM((PLANE, NZ, quarter, width), bf16) for _ in range(2)]
    scratch += [pltpu.VMEM((NZ * NY * NC, width, width), bf16) for _ in range(2)]
    scratch += [pltpu.VMEM(square, bf16) for _ in range(2)]
    scratch += [
        pltpu.VMEM((ITERS, NOCC, width), f32),
        pltpu.VMEM((ITERS, NOCC, width), f32),
        pltpu.VMEM((2 * ITERS, share, width), f32),
        pltpu.VMEM((ITERS, NY - 1, share, width), f32),
        pltpu.VMEM((ITERS, NX - 1, share, width), f32),
        pltpu.VMEM((ITERS, NZ - 1, share, width), f32),
        pltpu.VMEM((ITERS, 4, share, width), f32),
        pltpu.VMEM((per * nb, width, width), bf16),
        pltpu.VMEM(square, bf16),
        pltpu.VMEM(square, f32),
        pltpu.VMEM((per, width), f32),
        pltpu.VMEM((per, width), f32),
        pltpu.VMEM((nb, total), i32),
        pltpu.VMEM((total // width, width), i32),
        pltpu.VMEM(square, f32),
        pltpu.VMEM(square, f32),
        pltpu.VMEM(square, f32),
        pltpu.VMEM((NZ, width), i32),
        pltpu.VMEM((nb, width), i32),
        pltpu.SMEM((NZ, width), i32),
        pltpu.SMEM((nb, width), i32),
        pltpu.SMEM((per * nb,), i32),
        dma((9,)),
        dma((ITERS,)),
        dma((ITERS,)),
        dma((ITERS,)),
        dma((ITERS, 2 * NZ)),
        dma((ITERS,)),
        dma((ITERS,)),
        dma((ITERS, 5)),
        dma((ITERS, 5)),
    ]
    return pl.pallas_call(
        kernel,
        out_shape=(
            jax.ShapeDtypeStruct(square, f32),
            jax.ShapeDtypeStruct(square, f32),
        ),
        in_specs=[smem, smem, smem, hbm, hbm, hbm, hbm, hbm, hbm, hbm],
        out_specs=(vmem, vmem),
        scratch_shapes=scratch,
        compiler_params=pltpu.CompilerParams(
            collective_id=0, has_side_effects=True, vmem_limit_bytes=67043328
        ),
    )(
        couplings,
        pair_orbitals,
        pair_slot,
        amplitudes,
        integrals,
        energies,
        intersections.reshape(per * nb, width, width),
        projector,
        coupled.T,
        pair_slot.reshape(total // width, width),
    )


def solution(mesh):
    both = ("pairs", "orb")
    return jax.shard_map(
        body,
        mesh=mesh,
        in_specs=(
            P(both, None, None),
            P(both, None, None),
            P(both, None),
            P(both, None, None, None),
            P(both, None),
            P(both, None),
            P(both, None),
            P(),
            P(),
        ),
        out_specs=(P(both, None, None), P(both, None, None)),
        check_vma=False,
    )
```

time: 111 us -> 90.1 us (0.81)
  Pallas kernels: 96.3 us -> 84.6 us
  local copies, waits for them, and re-layouts: 11.2 us -> 4.68 us
  other arithmetic: 2.61 us -> 0 us
    pallas_call x1, Pallas kernels: 96.3 us -> 84.6 us  [body(): pl.pallas_call(kernel, out_shape=(jax.ShapeDtypeStruct(square, f32), jax....]
    unnamed x14 -> x3, local copies, waits for them, and re-layouts: 8.01 us -> 4.68 us
    gather x2 -> x0, local copies, waits for them, and re-layouts: 2.04 us -> none  [the longest x1 1.47 us: tables(): target = pair_slot[wanted[0]] // group]
    reduce_max x1 -> x0, other arithmetic: 1.38 us -> none  [tables(): jnp.max(jnp.where(held[:, None, :, None] == wanted[None, :, None, :], pla...]
where the time goes in v2:
time: 90.1 us; the launch traced here: 89.9 us
  Pallas kernels  84.6 us (94%)
  local copies, waits for them, and re-layouts  4.68 us (5%)
    pallas_call x1, Pallas kernels, body(): pl.pallas_call(kernel, out_shape=(jax.ShapeDtypeStruct(square, f32), jax....  84.6 us
    unnamed x3, local copies, waits for them, and re-layouts  4.68 us

profile of v2, /device:TPU:1, one launch (start us, length us, event | category | flops | bytes accessed | tf_op | source)
XLA Modules:
  0.0 89.9 jit_solution(10864292996814357266)
XLA Ops:
  0.6 1.3 %copy.11.orbs = s32[4,2]{1,0:T(4,128)} copy(s32[4,2]{0,1:T(2,128)} %param.15) | data formatting | bytes 64 | tf_op args[6]
  2.0 84.6 %shard_map.104 = (f32[4,128,128]{2,1,0:T(8,128)}, f32[4,128,128]{2,1,0:T(8,128)}) custom-call(f32[4,16]{1,0:T(4,128)} %coup.1, s32[4,2]{1,0:T(4,128)} %copy.11.orbs, s32[1024]{0:T(1024)} %slot_of.1, f32[4,128,128]{2,1,0:T(8,128)} %amp_hbm.1, bf16[4,128,128]{2,1,0:T(8,128)(2,1)} %integ_hbm.1, f32[4,128]{1,0:T(4,128)} %ener_hbm.1, ...), custom_call_target="tpu_custom_call" | custom-call | tf_op jit(solution)/shard_map/pallas_call | solution.py:373
  86.6 1.7 %copy.14 = f32[4,128,128]{2,1,0:T(8,128)} copy(f32[4,128,128]{2,1,0:T(8,128)} %get-tuple-element.4) | data formatting | bytes 524288
  88.3 1.7 %copy.15 = f32[4,128,128]{2,1,0:T(8,128)} copy(f32[4,128,128]{2,1,0:T(8,128)} %get-tuple-element.5) | data formatting | bytes 524288

commit v3 on v2

--- a/solution.py
+++ b/solution.py
@@ -20,14 +20,14 @@
 
 
 def kernel(
-    coup, orbs, slot_of, amp_hbm, integ_hbm, ener_hbm, inter_hbm, proj_hbm, coupled_hbm, slots_hbm, fin, res,
+    coup, orbs, slot_of, amp_hbm, integ_hbm, ener_hbm, inter_hbm, proj_hbm, coupled_hbm, slots_hbm, last_hbm, change_hbm,
     *scratch,
 ):
     gath = [scratch[0:NZ], scratch[NZ : 2 * NZ]]
     out_buf = scratch[2 * NZ : 2 * NZ + 2]
     recv = scratch[2 * NZ + 2 : 2 * NZ + 4]
     blocks = scratch[2 * NZ + 4 : 2 * NZ + 6]
-    (parts, full, half, part_y, part_x, part_z, sums, inter, integ, state, ener, proj, cpl, slots, den, pcol, base,
+    (parts, full, half, part_y, part_x, part_z, sums, inter, integ, state, ener, proj, cpl, slots, den, pcol, base, change,
      sel_v, want_v, sel, want, entry,
      local_sem, x_send, x_recv, z_send, z_recv, y_send, y_recv, p_send, p_recv) = scratch[2 * NZ + 6 :]
     per, width, _ = state.shape
@@ -47,6 +47,7 @@
         return (pair_index(ys[dy], zs[dz], cs[dc]), xs[dx])
 
     steps = [(dx, dy, dc) for dx in range(NX) for dy in range(NY) for dc in range(NC)]
+    far_first = sorted(steps, key=lambda t: -(min(t[0], NX - t[0]) + min(t[1], NY - t[1])))
 
     local = [
         pltpu.make_async_copy(a, b, local_sem.at[i])
@@ -168,8 +169,8 @@
                 preferred_element_type=jnp.float32,
             )[0:1]
             row = jnp.broadcast_to(row, (NOCC, width))
-            total += jnp.where(orbital == orbs[s, 0], row, 0.0)
-            total += jnp.where(orbital == orbs[s, 1], row, 0.0)
+            total += jnp.where(orbital == orbs[0, s], row, 0.0)
+            total += jnp.where(orbital == orbs[1, s], row, 0.0)
         parts[it] = total
 
     for it in range(ITERS):
@@ -193,7 +194,8 @@
                     out_buf[it][i, first + j] = g[k][sel[k, at]]
             for j in range(count):
                 recv[it][first + j, own_rows, :] = out_buf[it][0, first + j]
-            for i, (dx, dy, dc) in enumerate(steps):
+            for dx, dy, dc in far_first:
+                i = steps.index((dx, dy, dc))
                 if i:
                     send(
                         out_buf[it].at[i, pl.ds(first, count)],
@@ -279,8 +281,12 @@
                 e_row = ener[s : s + 1, :]
                 den[s] = column(e_row) + e_row
                 pcol[s] = column(proj[s : s + 1, :])
-        for s in range(per):
-            base[s] = integ[s].astype(jnp.float32) + den[s] * state[s]
+        if it == ITERS - 1:
+            last_copy = pltpu.make_async_copy(state, last_hbm, local_sem.at[len(local) + 3])
+            last_copy.start()
+        else:
+            for s in range(per):
+                base[s] = integ[s].astype(jnp.float32) + den[s] * state[s]
 
         arrived(half.at[ITERS + it], p_recv.at[it, 4])
         full[it, other, :] = half[ITERS + it]
@@ -290,21 +296,28 @@
 
         def one_slot(s, carry, it=it):
             acc = jnp.zeros((width, width), jnp.float32)
-            for k in range(nb):
-                own = inter[s * nb + k]
-                lifted = jnp.dot(own, recv[it][entry[s * nb + k]], preferred_element_type=jnp.float32)
-                scaled = (coup[s, k] * lifted).astype(jnp.bfloat16)
+            scaled = [
+                (
+                    coup[s, k]
+                    * jnp.dot(inter[s * nb + k], recv[it][entry[s * nb + k]], preferred_element_type=jnp.float32)
+                ).astype(jnp.bfloat16)
+                for k in range(nb)
+            ]
+            for k in range(0, nb, 2):
                 acc += lax.dot_general(
-                    scaled, own, (((1,), (1,)), ((), ())), preferred_element_type=jnp.float32
+                    jnp.concatenate(scaled[k : k + 2], axis=1),
+                    jnp.concatenate([inter[s * nb + k], inter[s * nb + k + 1]], axis=1),
+                    (((1,), (1,)), ((), ())),
+                    preferred_element_type=jnp.float32,
                 )
-            left_row = full[it, pl.ds(orbs[s, 0], 1), :]
-            right_row = full[it, pl.ds(orbs[s, 1], 1), :]
-            resid = base[s] - acc + column(left_row) * proj[pl.ds(s, 1), :] + pcol[s] * right_row
-            new = state[s] - resid / den[s]
+            left_row = full[it, pl.ds(orbs[0, s], 1), :]
+            right_row = full[it, pl.ds(orbs[1, s], 1), :]
+            added = column(left_row) * proj[pl.ds(s, 1), :] + pcol[s] * right_row - acc
             if it == ITERS - 1:
-                res[s] = resid
-                fin[s] = new
+                change[s] = added
+                pltpu.make_async_copy(change.at[s], change_hbm.at[s], local_sem.at[len(local) + 2]).start()
             else:
+                new = state[s] - (base[s] + added) / den[s]
                 state[s] = new
                 blocks[it + 1][s] = new.astype(jnp.bfloat16)
                 spread(it + 1, s)
@@ -312,6 +325,8 @@
 
         lax.fori_loop(0, per, one_slot, 0)
 
+    last_copy.wait()
+    pltpu.make_async_copy(change, change_hbm, local_sem.at[len(local) + 2]).wait()
     for copy in sent:
         copy.wait_send()
     for it in range(ITERS):
@@ -327,7 +342,6 @@
     group = NX * per
     quarter = width // NX
     bf16, f32, i32 = jnp.bfloat16, jnp.float32, jnp.int32
-    vmem = pl.BlockSpec(memory_space=pltpu.VMEM)
     smem = pl.BlockSpec(memory_space=pltpu.SMEM)
     hbm = pl.BlockSpec(memory_space=pltpu.HBM)
     dma = pltpu.SemaphoreType.DMA
@@ -355,12 +369,13 @@
         pltpu.VMEM(square, f32),
         pltpu.VMEM(square, f32),
         pltpu.VMEM(square, f32),
+        pltpu.VMEM(square, f32),
         pltpu.VMEM((NZ, width), i32),
         pltpu.VMEM((nb, width), i32),
         pltpu.SMEM((NZ, width), i32),
         pltpu.SMEM((nb, width), i32),
         pltpu.SMEM((per * nb,), i32),
-        dma((9,)),
+        dma((11,)),
         dma((ITERS,)),
         dma((ITERS,)),
         dma((ITERS,)),
@@ -370,21 +385,21 @@
         dma((ITERS, 5)),
         dma((ITERS, 5)),
     ]
-    return pl.pallas_call(
+    last, change = pl.pallas_call(
         kernel,
         out_shape=(
             jax.ShapeDtypeStruct(square, f32),
             jax.ShapeDtypeStruct(square, f32),
         ),
         in_specs=[smem, smem, smem, hbm, hbm, hbm, hbm, hbm, hbm, hbm],
-        out_specs=(vmem, vmem),
+        out_specs=(hbm, hbm),
         scratch_shapes=scratch,
         compiler_params=pltpu.CompilerParams(
             collective_id=0, has_side_effects=True, vmem_limit_bytes=67043328
         ),
     )(
         couplings,
-        pair_orbitals,
+        pair_orbitals.T,
         pair_slot,
         amplitudes,
         integrals,
@@ -394,6 +409,9 @@
         coupled.T,
         pair_slot.reshape(total // width, width),
     )
+    denom = energies[:, :, None] + energies[:, None, :]
+    residual = integrals.astype(f32) + denom * last + change
+    return (last - residual / denom, residual)
 
 
 def solution(mesh):

time: 90.1 us -> 81.2 us (0.901)
  Pallas kernels: 84.6 us -> 78.4 us
  local copies, waits for them, and re-layouts: 4.68 us -> 0 us
  other arithmetic: 0 us -> 2.02 us
    pallas_call x1, Pallas kernels: 84.6 us -> 78.4 us  [body(): pl.pallas_call(kernel, out_shape=(jax.ShapeDtypeStruct(square, f32), jax....]
    unnamed x3 -> x0, local copies, waits for them, and re-layouts: 4.68 us -> none
    sub x0 -> x1, other arithmetic: none -> 2.02 us  [body(): return (last - residual / denom, residual)]
where the time goes in v3:
time: 81.2 us; the launch traced here: 81 us
  Pallas kernels  78.4 us (97%)
  other arithmetic  2.02 us (2%)
    pallas_call x1, Pallas kernels, body(): pl.pallas_call(kernel, out_shape=(jax.ShapeDtypeStruct(square, f32), jax....  78.4 us
    sub x1, other arithmetic, body(): return (last - residual / denom, residual)  2.02 us

profile of v3, /device:TPU:1, one launch (start us, length us, event | category | flops | bytes accessed | tf_op | source)
XLA Modules:
  0.0 81.0 jit_solution(2070121618512403956)
XLA Ops:
  0.6 78.4 %shard_map.104 = (f32[4,128,128]{2,1,0:T(8,128)}, f32[4,128,128]{2,1,0:T(8,128)}) custom-call(f32[4,16]{1,0:T(4,128)} %coup.1, s32[2,4]{1,0:T(2,128)} %bitcast.7, s32[1024]{0:T(1024)} %slot_of.1, f32[4,128,128]{2,1,0:T(8,128)} %amp_hbm.1, bf16[4,128,128]{2,1,0:T(8,128)(2,1)} %integ_hbm.1, f32[4,128]{1,0:T(4,128)} %ener_hbm.1, bf16[64,128,128]{2,1,0:T(8,128)(2,1)} %bitcast.4, ...), custom_call_target="tpu_custom_call" | custom-call | tf_op jit(solution)/shard_map/pallas_call | solution.py:388
  79.0 2.0 %fusion.2 = (f32[4,128,128]{2,1,0:T(8,128)}, f32[4,128,128]{2,1,0:T(8,128)}) fusion(f32[4,128,128]{2,1,0:T(8,128)} %get-tuple-element.4, f32[4,128]{1,0:T(4,128)} %ener_hbm.1, f32[4,128,128]{2,1,0:T(8,128)} %get-tuple-element.5, bf16[4,128,128]{2,1,0:T(8,128)(2,1)} %integ_hbm.1), kind=kLoop, calls=%fused_computation.4 | loop fusion | flops 458752 | bytes 1181696 | tf_op jit(solution)/shard_map/sub | solution.py:414

commit v4 on v3

--- a/solution.py
+++ b/solution.py
@@ -27,7 +27,7 @@
     out_buf = scratch[2 * NZ : 2 * NZ + 2]
     recv = scratch[2 * NZ + 2 : 2 * NZ + 4]
     blocks = scratch[2 * NZ + 4 : 2 * NZ + 6]
-    (parts, full, half, part_y, part_x, part_z, sums, inter, integ, state, ener, proj, cpl, slots, den, pcol, base, change,
+    (parts, full, half, part_y, part_x, part_z, sums, inter, integ, state, ener, proj, cpl, slots, den, rden, pcol, base, change,
      sel_v, want_v, sel, want, entry,
      local_sem, x_send, x_recv, z_send, z_recv, y_send, y_recv, p_send, p_recv) = scratch[2 * NZ + 6 :]
     per, width, _ = state.shape
@@ -68,10 +68,10 @@
 
     barrier = pltpu.get_barrier_semaphore()
 
-    for d in range(1, NZ):
-        pl.semaphore_signal(barrier, inc=1, device_id=dev(dz=d), device_id_type=MESH)
-    for dx, dy, dc in steps[1:]:
-        pl.semaphore_signal(barrier, inc=1, device_id=dev(dx, dy, 0, dc), device_id_type=MESH)
+    up, down = dev(dz=1), dev(dz=NZ - 1)
+    peers = [up, down] + [dev(dx, dy, 0, dc) for dx, dy, dc in far_first if (dx, dy, dc) != (0, 0, 0)]
+    for peer in peers:
+        pl.semaphore_signal(barrier, inc=1, device_id=peer, device_id_type=MESH)
 
     local[0].wait()
     for s in range(per):
@@ -114,9 +114,10 @@
         while shift:
             held += pltpu.roll(held, shift, 1)
             shift //= 2
+        place = (row % group // per + NX - x) % NX * per + row % per
         hits = jnp.zeros((width, width), jnp.int32)
         for e in range(nb):
-            hits = jnp.maximum(hits, jnp.where(wanted[e : e + 1, :] == held, row % group, 0))
+            hits = jnp.maximum(hits, jnp.where(wanted[e : e + 1, :] == held, place, 0))
         best = hits
         for r in range(1, per):
             best = jnp.maximum(best, pltpu.roll(hits, width - r, 1))
@@ -144,16 +145,16 @@
     own_rows = pl.ds(pl.multiple_of(x * quarter, quarter), quarter)
 
     def spread(it, s):
-        for d in range(1, NX):
+        gath[it][0][s] = blocks[it][s, own_rows, :]
+        for d in (1, 3, 2):
             theirs = pl.ds(pl.multiple_of(xs[d] * quarter, quarter), quarter)
             send(
                 blocks[it].at[s, theirs],
-                gath[it][0].at[x * per + s],
+                gath[it][0].at[(NX - d) * per + s],
                 x_send.at[it],
-                x_recv.at[it],
+                x_recv.at[it, NX - d],
                 dev(dx=d),
             )
-        gath[it][0][x * per + s] = blocks[it][s, own_rows, :]
 
     def singles_terms(it):
         if it == 0:
@@ -176,14 +177,22 @@
     for it in range(ITERS):
         g = gath[it]
 
-        def push(k, h, k2, to, g=g, it=it):
-            def part(j):
-                return g[j].at[pl.ds(h * (group // 2), group // 2)]
-
-            sent.append(send(part(k), part(k2), z_send.at[it], z_recv.at[it, k2 * 2 + h], to))
-
-        def ready(k, h, g=g, it=it):
-            arrived(g[k].at[pl.ds(h * (group // 2), group // 2)], z_recv.at[it, k * 2 + h])
+        def piece(k, q, g=g):
+            return g[k].at[pl.ds(q * per, per)]
+
+        def push(k, q, k2, to, piece=piece, it=it):
+            sent.append(send(piece(k, q), piece(k2, q), z_send.at[it], z_recv.at[it, k2 * NX + q], to))
+
+        def ready(k, q, piece=piece, it=it):
+            arrived(piece(k, q), z_recv.at[it, k * NX + q])
+
+        def ring(k, k2, to, it=it):
+            sent.append(
+                send(part_z.at[it, k], part_z.at[it, k2], p_send.at[it, 3], p_recv.at[it, 3 + k2], to)
+            )
+
+        def ringed(k, it=it):
+            arrived(part_z.at[it, k], p_recv.at[it, 3 + k])
 
         def deliver(ks, it=it, g=g):
             first, count = FIRST[ks[0]], len(ks)
@@ -208,88 +217,101 @@
         if it == 0:
             singles_terms(0)
             make_tables()
-            pl.semaphore_wait(barrier, PLANE - 1 + NZ - 1)
+            pl.semaphore_wait(barrier, len(peers))
             for s in range(per):
                 spread(0, s)
-        else:
+        push(0, 0, 1, up)
+        push(0, 0, 7, down)
+        if it:
             singles_terms(it)
         share = NOCC // NC
         mine = pl.ds(pl.multiple_of(c * share, share), share)
         other = pl.ds(pl.multiple_of((1 - c) * share, share), share)
         sent.append(send(parts.at[it, other], half.at[it], p_send.at[it, 0], p_recv.at[it, 0], dev(dc=1)))
 
-        up, down = dev(dz=1), dev(dz=NZ - 1)
-        arrived(g[0].at[pl.ds(0, group - per)], x_recv.at[it])
-        for h in range(2):
-            push(0, h, 1, up)
-            push(0, h, 7, down)
-        deliver((0,))
-
+        for q in (1, 3, 2):
+            arrived(piece(0, q), x_recv.at[it, q])
+            push(0, q, 1, up)
+            push(0, q, 7, down)
         arrived(half.at[it], p_recv.at[it, 0])
         sums[it, 0] = parts[it, mine, :] + half[it]
         for d in range(1, NY):
             sent.append(send(sums.at[it, 0], part_y.at[it, d - 1], p_send.at[it, 1], p_recv.at[it, 1], dev(dy=d)))
-
-        for h in range(2):
-            ready(1, h)
-            push(1, h, 2, up)
-            ready(7, h)
-            push(7, h, 6, down)
-        deliver((1, 7))
-
+        deliver((0,))
+
+        for q in (0, 1, 3, 2):
+            ready(1, q)
+            push(1, q, 2, up)
+            ready(7, q)
+            push(7, q, 6, down)
         arrived(part_y.at[it], p_recv.at[it, 1])
         sums[it, 1] = sums[it, 0] + part_y[it, 0] + part_y[it, 1] + part_y[it, 2]
         for d in range(1, NX):
             sent.append(send(sums.at[it, 1], part_x.at[it, d - 1], p_send.at[it, 2], p_recv.at[it, 2], dev(dx=d)))
-
-        for h in range(2):
-            ready(2, h)
-            push(2, h, 3, up)
-            ready(6, h)
-            push(6, h, 5, down)
+        deliver((1, 7))
+
+        for q in (0, 1, 3, 2):
+            ready(2, q)
+            push(2, q, 3, up)
+            ready(6, q)
+            push(6, q, 5, down)
+        arrived(part_x.at[it], p_recv.at[it, 2])
+        part_z[it, 0] = sums[it, 1] + part_x[it, 0] + part_x[it, 1] + part_x[it, 2]
+        ring(0, 1, up)
+        ring(0, 7, down)
         deliver((2, 6))
 
-        arrived(part_x.at[it], p_recv.at[it, 2])
-        sums[it, 2] = sums[it, 1] + part_x[it, 0] + part_x[it, 1] + part_x[it, 2]
-        for d in range(1, NZ):
-            sent.append(send(sums.at[it, 2], part_z.at[it, d - 1], p_send.at[it, 3], p_recv.at[it, 3], dev(dz=d)))
-
-        ready(3, 0)
-        push(3, 0, 4, up)
-        ready(5, 1)
-        push(5, 1, 4, down)
-        ready(5, 0)
-        ready(3, 1)
+        for q in (0, 1, 3, 2):
+            ready(3, q)
+            if q in (0, 1):
+                push(3, q, 4, up)
+            ready(5, q)
+            if q in (2, 3):
+                push(5, q, 4, down)
+        ringed(1)
+        ring(1, 2, up)
+        ringed(7)
+        ring(7, 6, down)
         deliver((3, 5))
-        ready(4, 0)
-        ready(4, 1)
+        for q in (0, 1, 3, 2):
+            ready(4, q)
         deliver((4,))
 
-        arrived(part_z.at[it], p_recv.at[it, 3])
-        total = sums[it, 2]
-        for i in range(NZ - 1):
-            total += part_z[it, i]
-        full[it, mine, :] = total
-        sums[it, 3] = total
-        sent.append(send(sums.at[it, 3], half.at[ITERS + it], p_send.at[it, 4], p_recv.at[it, 4], dev(dc=1)))
-
+        ringed(2)
+        ring(2, 3, up)
+        ringed(6)
+        ring(6, 5, down)
         if it == 0:
             make_entries()
             local[4].wait()
-            local[5].wait()
             for s in range(per):
                 e_row = ener[s : s + 1, :]
                 den[s] = column(e_row) + e_row
+                rden[s] = 1.0 / den[s]
                 pcol[s] = column(proj[s : s + 1, :])
+            local[5].wait()
+        ringed(3)
+        ring(3, 4, up)
+        ringed(5)
+        ringed(4)
+        total = part_z[it, 0]
+        for k in range(1, NZ):
+            total += part_z[it, k]
+        full[it, mine, :] = total
+        sums[it, 2] = total
+        sent.append(send(sums.at[it, 2], half.at[ITERS + it], p_send.at[it, 4], p_recv.at[it, 2 * NX + 3], dev(dc=1)))
+        arrived(half.at[ITERS + it], p_recv.at[it, 2 * NX + 3])
+        full[it, other, :] = half[ITERS + it]
         if it == ITERS - 1:
             last_copy = pltpu.make_async_copy(state, last_hbm, local_sem.at[len(local) + 3])
             last_copy.start()
-        else:
-            for s in range(per):
-                base[s] = integ[s].astype(jnp.float32) + den[s] * state[s]
-
-        arrived(half.at[ITERS + it], p_recv.at[it, 4])
-        full[it, other, :] = half[ITERS + it]
+        for s in range(per):
+            left_row = full[it, pl.ds(orbs[0, s], 1), :]
+            right_row = full[it, pl.ds(orbs[1, s], 1), :]
+            base[s] = column(left_row) * proj[s : s + 1, :] + pcol[s] * right_row
+            if it < ITERS - 1:
+                whole = integ[s].astype(jnp.float32) + den[s] * state[s] + base[s]
+                base[s] = state[s] - whole / den[s]
         if it == 0:
             local[6].wait()
         arrived(recv[it].at[pl.ds(0, (PLANE - 1) * NZ // NX)], y_recv.at[it])
@@ -310,14 +332,11 @@
                     (((1,), (1,)), ((), ())),
                     preferred_element_type=jnp.float32,
                 )
-            left_row = full[it, pl.ds(orbs[0, s], 1), :]
-            right_row = full[it, pl.ds(orbs[1, s], 1), :]
-            added = column(left_row) * proj[pl.ds(s, 1), :] + pcol[s] * right_row - acc
             if it == ITERS - 1:
-                change[s] = added
+                change[s] = base[s] - acc
                 pltpu.make_async_copy(change.at[s], change_hbm.at[s], local_sem.at[len(local) + 2]).start()
             else:
-                new = state[s] - (base[s] + added) / den[s]
+                new = base[s] + acc * rden[s]
                 state[s] = new
                 blocks[it + 1][s] = new.astype(jnp.bfloat16)
                 spread(it + 1, s)
@@ -357,7 +376,7 @@
         pltpu.VMEM((2 * ITERS, share, width), f32),
         pltpu.VMEM((ITERS, NY - 1, share, width), f32),
         pltpu.VMEM((ITERS, NX - 1, share, width), f32),
-        pltpu.VMEM((ITERS, NZ - 1, share, width), f32),
+        pltpu.VMEM((ITERS, NZ, share, width), f32),
         pltpu.VMEM((ITERS, 4, share, width), f32),
         pltpu.VMEM((per * nb, width, width), bf16),
         pltpu.VMEM(square, bf16),
@@ -366,6 +385,7 @@
         pltpu.VMEM((per, width), f32),
         pltpu.VMEM((nb, total), i32),
         pltpu.VMEM((total // width, width), i32),
+        pltpu.VMEM(square, f32),
         pltpu.VMEM(square, f32),
         pltpu.VMEM(square, f32),
         pltpu.VMEM(square, f32),
@@ -377,13 +397,13 @@
         pltpu.SMEM((per * nb,), i32),
         dma((11,)),
         dma((ITERS,)),
+        dma((ITERS, NX)),
         dma((ITERS,)),
-        dma((ITERS,)),
-        dma((ITERS, 2 * NZ)),
+        dma((ITERS, NX * NZ)),
         dma((ITERS,)),
         dma((ITERS,)),
         dma((ITERS, 5)),
-        dma((ITERS, 5)),
+        dma((ITERS, NZ + 4)),
     ]
     last, change = pl.pallas_call(
         kernel,

time: 81.2 us -> 79.6 us (0.980)
  Pallas kernels: 78.4 us -> 76.7 us
    pallas_call x1, Pallas kernels: 78.4 us -> 76.7 us  [body(): pl.pallas_call(kernel, out_shape=(jax.ShapeDtypeStruct(square, f32), jax....]
where the time goes in v4:
time: 79.6 us; the launch traced here: 79.4 us
  Pallas kernels  76.7 us (96%)
  other arithmetic  2.02 us (3%)
    pallas_call x1, Pallas kernels, body(): pl.pallas_call(kernel, out_shape=(jax.ShapeDtypeStruct(square, f32), jax....  76.7 us
    sub x1, other arithmetic, body(): return (last - residual / denom, residual)  2.02 us

profile of v4, /device:TPU:1, one launch (start us, length us, event | category | flops | bytes accessed | tf_op | source)
XLA Modules:
  0.0 79.4 jit_solution(13099298488044821179)
XLA Ops:
  0.6 76.7 %shard_map.104 = (f32[4,128,128]{2,1,0:T(8,128)}, f32[4,128,128]{2,1,0:T(8,128)}) custom-call(f32[4,16]{1,0:T(4,128)} %coup.1, s32[2,4]{1,0:T(2,128)} %bitcast.7, s32[1024]{0:T(1024)} %slot_of.1, f32[4,128,128]{2,1,0:T(8,128)} %amp_hbm.1, bf16[4,128,128]{2,1,0:T(8,128)(2,1)} %integ_hbm.1, f32[4,128]{1,0:T(4,128)} %ener_hbm.1, bf16[64,128,128]{2,1,0:T(8,128)(2,1)} %bitcast.4, ...), custom_call_target="tpu_custom_call" | custom-call | tf_op jit(solution)/shard_map/pallas_call | solution.py:408
  77.4 2.0 %fusion.2 = (f32[4,128,128]{2,1,0:T(8,128)}, f32[4,128,128]{2,1,0:T(8,128)}) fusion(f32[4,128,128]{2,1,0:T(8,128)} %get-tuple-element.4, f32[4,128]{1,0:T(4,128)} %ener_hbm.1, f32[4,128,128]{2,1,0:T(8,128)} %get-tuple-element.5, bf16[4,128,128]{2,1,0:T(8,128)(2,1)} %integ_hbm.1), kind=kLoop, calls=%fused_computation.4 | loop fusion | flops 458752 | bytes 1181696 | tf_op jit(solution)/shard_map/sub | solution.py:434

commit v5 on v4

--- a/solution.py
+++ b/solution.py
@@ -11,8 +11,8 @@
 PLANE = NX * NY * NC
 MESH = pl.DeviceIdType.MESH
 HIGHEST = lax.Precision.HIGHEST
-ROUNDS = ((0,), (1, 7), (2, 6), (3, 5), (4,))
-FIRST = {0: 0, 1: 1, 2: 3, 3: 5, 4: 7}
+ROUNDS = ((0,), (1, 7), (2, 6), (3, 5, 4))
+FIRST = {0: 0, 1: 1, 2: 3, 3: 5}
 
 
 def pair_index(y, z, c):
@@ -29,7 +29,7 @@
     blocks = scratch[2 * NZ + 4 : 2 * NZ + 6]
     (parts, full, half, part_y, part_x, part_z, sums, inter, integ, state, ener, proj, cpl, slots, den, rden, pcol, base, change,
      sel_v, want_v, sel, want, entry,
-     local_sem, x_send, x_recv, z_send, z_recv, y_send, y_recv, p_send, p_recv) = scratch[2 * NZ + 6 :]
+     local_sem, x_send, z_send, z_recv, y_send, y_recv, p_send, p_recv) = scratch[2 * NZ + 6 :]
     per, width, _ = state.shape
     nb = inter.shape[0] // per
     group = NX * per
@@ -69,7 +69,8 @@
     barrier = pltpu.get_barrier_semaphore()
 
     up, down = dev(dz=1), dev(dz=NZ - 1)
-    peers = [up, down] + [dev(dx, dy, 0, dc) for dx, dy, dc in far_first if (dx, dy, dc) != (0, 0, 0)]
+    peers = [up, down]
+    peers += [dev(dx, dy, 0, dc) for dx, dy, dc in far_first if (dx, dy, dc) != (0, 0, 0)]
     for peer in peers:
         pl.semaphore_signal(barrier, inc=1, device_id=peer, device_id_type=MESH)
 
@@ -144,17 +145,18 @@
 
     own_rows = pl.ds(pl.multiple_of(x * quarter, quarter), quarter)
 
-    def spread(it, s):
-        gath[it][0][s] = blocks[it][s, own_rows, :]
+    def spread(it, s, count=1):
+        slots_in = pl.ds(s, count)
         for d in (1, 3, 2):
             theirs = pl.ds(pl.multiple_of(xs[d] * quarter, quarter), quarter)
             send(
-                blocks[it].at[s, theirs],
-                gath[it][0].at[(NX - d) * per + s],
+                blocks[it].at[slots_in, theirs],
+                gath[it][0].at[pl.ds((NX - d) * per + s, count)],
                 x_send.at[it],
-                x_recv.at[it, NX - d],
+                z_recv.at[it, NX - d],
                 dev(dx=d),
             )
+        gath[it][0][slots_in] = blocks[it][slots_in, own_rows, :]
 
     def singles_terms(it):
         if it == 0:
@@ -218,8 +220,7 @@
             singles_terms(0)
             make_tables()
             pl.semaphore_wait(barrier, len(peers))
-            for s in range(per):
-                spread(0, s)
+            spread(0, 0, per)
         push(0, 0, 1, up)
         push(0, 0, 7, down)
         if it:
@@ -230,7 +231,7 @@
         sent.append(send(parts.at[it, other], half.at[it], p_send.at[it, 0], p_recv.at[it, 0], dev(dc=1)))
 
         for q in (1, 3, 2):
-            arrived(piece(0, q), x_recv.at[it, q])
+            ready(0, q)
             push(0, q, 1, up)
             push(0, q, 7, down)
         arrived(half.at[it], p_recv.at[it, 0])
@@ -272,10 +273,9 @@
         ring(1, 2, up)
         ringed(7)
         ring(7, 6, down)
-        deliver((3, 5))
         for q in (0, 1, 3, 2):
             ready(4, q)
-        deliver((4,))
+        deliver((3, 5, 4))
 
         ringed(2)
         ring(2, 3, up)
@@ -316,7 +316,7 @@
             local[6].wait()
         arrived(recv[it].at[pl.ds(0, (PLANE - 1) * NZ // NX)], y_recv.at[it])
 
-        def one_slot(s, carry, it=it):
+        def one_slot(s, it=it):
             acc = jnp.zeros((width, width), jnp.float32)
             scaled = [
                 (
@@ -340,9 +340,9 @@
                 state[s] = new
                 blocks[it + 1][s] = new.astype(jnp.bfloat16)
                 spread(it + 1, s)
-            return carry
-
-        lax.fori_loop(0, per, one_slot, 0)
+
+        for s in range(per):
+            one_slot(s)
 
     last_copy.wait()
     pltpu.make_async_copy(change, change_hbm, local_sem.at[len(local) + 2]).wait()
@@ -397,7 +397,6 @@
         pltpu.SMEM((per * nb,), i32),
         dma((11,)),
         dma((ITERS,)),
-        dma((ITERS, NX)),
         dma((ITERS,)),
         dma((ITERS, NX * NZ)),
         dma((ITERS,)),

time: 79.6 us -> 78 us (0.980)
  Pallas kernels: 76.7 us -> 75.1 us
    pallas_call x1, Pallas kernels: 76.7 us -> 75.1 us  [body(): pl.pallas_call(kernel, out_shape=(jax.ShapeDtypeStruct(square, f32), jax....]
where the time goes in v5:
time: 78 us; the launch traced here: 77.8 us
  Pallas kernels  75.1 us (96%)
  other arithmetic  2.02 us (3%)
    pallas_call x1, Pallas kernels, body(): pl.pallas_call(kernel, out_shape=(jax.ShapeDtypeStruct(square, f32), jax....  75.1 us
    sub x1, other arithmetic, body(): return (last - residual / denom, residual)  2.02 us

profile of v5, /device:TPU:1, one launch (start us, length us, event | category | flops | bytes accessed | tf_op | source)
XLA Modules:
  0.0 77.8 jit_solution(1784604591311936904)
XLA Ops:
  0.6 75.1 %shard_map.104 = (f32[4,128,128]{2,1,0:T(8,128)}, f32[4,128,128]{2,1,0:T(8,128)}) custom-call(f32[4,16]{1,0:T(4,128)} %coup.1, s32[2,4]{1,0:T(2,128)} %bitcast.7, s32[1024]{0:T(1024)} %slot_of.1, f32[4,128,128]{2,1,0:T(8,128)} %amp_hbm.1, bf16[4,128,128]{2,1,0:T(8,128)(2,1)} %integ_hbm.1, f32[4,128]{1,0:T(4,128)} %ener_hbm.1, bf16[64,128,128]{2,1,0:T(8,128)(2,1)} %bitcast.4, ...), custom_call_target="tpu_custom_call" | custom-call | tf_op jit(solution)/shard_map/pallas_call | solution.py:407
  75.8 2.0 %fusion.2 = (f32[4,128,128]{2,1,0:T(8,128)}, f32[4,128,128]{2,1,0:T(8,128)}) fusion(f32[4,128,128]{2,1,0:T(8,128)} %get-tuple-element.4, f32[4,128]{1,0:T(4,128)} %ener_hbm.1, f32[4,128,128]{2,1,0:T(8,128)} %get-tuple-element.5, bf16[4,128,128]{2,1,0:T(8,128)(2,1)} %integ_hbm.1), kind=kLoop, calls=%fused_computation.4 | loop fusion | flops 458752 | bytes 1181696 | tf_op jit(solution)/shard_map/sub | solution.py:433

commit v6 on v5

--- a/solution.py
+++ b/solution.py
@@ -20,7 +20,7 @@
 
 
 def kernel(
-    coup, orbs, slot_of, amp_hbm, integ_hbm, ener_hbm, inter_hbm, proj_hbm, coupled_hbm, slots_hbm, last_hbm, change_hbm,
+    coup_hbm, orbs_hbm, slot_hbm, amp_hbm, integ_hbm, ener_hbm, inter_hbm, proj_hbm, coupled_hbm, slots_hbm, last_hbm, change_hbm,
     *scratch,
 ):
     gath = [scratch[0:NZ], scratch[NZ : 2 * NZ]]
@@ -28,7 +28,7 @@
     recv = scratch[2 * NZ + 2 : 2 * NZ + 4]
     blocks = scratch[2 * NZ + 4 : 2 * NZ + 6]
     (parts, full, half, part_y, part_x, part_z, sums, inter, integ, state, ener, proj, cpl, slots, den, rden, pcol, base, change,
-     sel_v, want_v, sel, want, entry,
+     sel_v, want_v, sel, want, entry, coup, orbs, slot_of,
      local_sem, x_send, z_send, z_recv, y_send, y_recv, p_send, p_recv) = scratch[2 * NZ + 6 :]
     per, width, _ = state.shape
     nb = inter.shape[0] // per
@@ -60,6 +60,9 @@
                 (ener_hbm, ener),
                 (integ_hbm, integ),
                 (inter_hbm, inter),
+                (orbs_hbm, orbs),
+                (slot_hbm, slot_of),
+                (coup_hbm, coup),
             )
         )
     ]
@@ -161,6 +164,7 @@
     def singles_terms(it):
         if it == 0:
             local[3].wait()
+            local[7].wait()
         orbital = lax.broadcasted_iota(jnp.int32, (NOCC, width), 0)
         total = jnp.zeros((NOCC, width), jnp.float32)
         for s in range(per):
@@ -282,6 +286,8 @@
         ringed(6)
         ring(6, 5, down)
         if it == 0:
+            local[8].wait()
+            local[9].wait()
             make_entries()
             local[4].wait()
             for s in range(per):
@@ -395,7 +401,10 @@
         pltpu.SMEM((NZ, width), i32),
         pltpu.SMEM((nb, width), i32),
         pltpu.SMEM((per * nb,), i32),
-        dma((11,)),
+        pltpu.SMEM((per, nb), f32),
+        pltpu.SMEM((2, per), i32),
+        pltpu.SMEM((total,), i32),
+        dma((14,)),
         dma((ITERS,)),
         dma((ITERS,)),
         dma((ITERS, NX * NZ)),
@@ -410,7 +419,7 @@
             jax.ShapeDtypeStruct(square, f32),
             jax.ShapeDtypeStruct(square, f32),
         ),
-        in_specs=[smem, smem, smem, hbm, hbm, hbm, hbm, hbm, hbm, hbm],
+        in_specs=[hbm, hbm, hbm, hbm, hbm, hbm, hbm, hbm, hbm, hbm],
         out_specs=(hbm, hbm),
         scratch_shapes=scratch,
         compiler_params=pltpu.CompilerParams(

time: 78 us -> 77.2 us (0.990)
  no operation moved by 1% of the time
where the time goes in v6:
time: 77.2 us; the launch traced here: 77.1 us
  Pallas kernels  74.4 us (96%)
  other arithmetic  2.02 us (3%)
    pallas_call x1, Pallas kernels, body(): pl.pallas_call(kernel, out_shape=(jax.ShapeDtypeStruct(square, f32), jax....  74.4 us
    sub x1, other arithmetic, body(): return (last - residual / denom, residual)  2.02 us

profile of v6, /device:TPU:1, one launch (start us, length us, event | category | flops | bytes accessed | tf_op | source)
XLA Modules:
  0.0 77.1 jit_solution(4517602826711658300)
XLA Ops:
  0.6 74.4 %shard_map.104 = (f32[4,128,128]{2,1,0:T(8,128)}, f32[4,128,128]{2,1,0:T(8,128)}) custom-call(f32[4,16]{1,0:T(4,128)} %coup_hbm.1, s32[2,4]{1,0:T(2,128)} %bitcast.7, s32[1024]{0:T(1024)} %slot_hbm.1, f32[4,128,128]{2,1,0:T(8,128)} %amp_hbm.1, bf16[4,128,128]{2,1,0:T(8,128)(2,1)} %integ_hbm.1, f32[4,128]{1,0:T(4,128)} %ener_hbm.1, ...), custom_call_target="tpu_custom_call" | custom-call | tf_op jit(solution)/shard_map/pallas_call | solution.py:416
  75.0 2.0 %fusion.2 = (f32[4,128,128]{2,1,0:T(8,128)}, f32[4,128,128]{2,1,0:T(8,128)}) fusion(f32[4,128,128]{2,1,0:T(8,128)} %get-tuple-element.4, f32[4,128]{1,0:T(4,128)} %ener_hbm.1, f32[4,128,128]{2,1,0:T(8,128)} %get-tuple-element.5, bf16[4,128,128]{2,1,0:T(8,128)(2,1)} %integ_hbm.1), kind=kLoop, calls=%fused_computation.4 | loop fusion | flops 458752 | bytes 1181696 | tf_op jit(solution)/shard_map/sub | solution.py:442

commit v7 on v6

--- a/solution.py
+++ b/solution.py
@@ -222,7 +222,6 @@
 
         if it == 0:
             singles_terms(0)
-            make_tables()
             pl.semaphore_wait(barrier, len(peers))
             spread(0, 0, per)
         push(0, 0, 1, up)
@@ -233,6 +232,8 @@
         mine = pl.ds(pl.multiple_of(c * share, share), share)
         other = pl.ds(pl.multiple_of((1 - c) * share, share), share)
         sent.append(send(parts.at[it, other], half.at[it], p_send.at[it, 0], p_recv.at[it, 0], dev(dc=1)))
+        if it == 0:
+            make_tables()
 
         for q in (1, 3, 2):
             ready(0, q)

time: 77.2 us -> 76.9 us (level)
  no operation moved by 1% of the time
where the time goes in v7:
time: 76.9 us; the launch traced here: 76.8 us
  Pallas kernels  74.1 us (96%)
  other arithmetic  2.02 us (3%)
    pallas_call x1, Pallas kernels, body(): pl.pallas_call(kernel, out_shape=(jax.ShapeDtypeStruct(square, f32), jax....  74.1 us
    sub x1, other arithmetic, body(): return (last - residual / denom, residual)  2.02 us

profile of v7, /device:TPU:1, one launch (start us, length us, event | category | flops | bytes accessed | tf_op | source)
XLA Modules:
  0.0 76.8 jit_solution(692567758803222299)
XLA Ops:
  0.6 74.1 %shard_map.104 = (f32[4,128,128]{2,1,0:T(8,128)}, f32[4,128,128]{2,1,0:T(8,128)}) custom-call(f32[4,16]{1,0:T(4,128)} %coup_hbm.1, s32[2,4]{1,0:T(2,128)} %bitcast.7, s32[1024]{0:T(1024)} %slot_hbm.1, f32[4,128,128]{2,1,0:T(8,128)} %amp_hbm.1, bf16[4,128,128]{2,1,0:T(8,128)(2,1)} %integ_hbm.1, f32[4,128]{1,0:T(4,128)} %ener_hbm.1, ...), custom_call_target="tpu_custom_call" | custom-call | tf_op jit(solution)/shard_map/pallas_call | solution.py:417
  74.8 2.0 %fusion.2 = (f32[4,128,128]{2,1,0:T(8,128)}, f32[4,128,128]{2,1,0:T(8,128)}) fusion(f32[4,128,128]{2,1,0:T(8,128)} %get-tuple-element.4, f32[4,128]{1,0:T(4,128)} %ener_hbm.1, f32[4,128,128]{2,1,0:T(8,128)} %get-tuple-element.5, bf16[4,128,128]{2,1,0:T(8,128)(2,1)} %integ_hbm.1), kind=kLoop, calls=%fused_computation.4 | loop fusion | flops 458752 | bytes 1181696 | tf_op jit(solution)/shard_map/sub | solution.py:443

commit v8 on v7

--- a/solution.py
+++ b/solution.py
@@ -325,13 +325,17 @@
 
         def one_slot(s, it=it):
             acc = jnp.zeros((width, width), jnp.float32)
-            scaled = [
-                (
-                    coup[s, k]
-                    * jnp.dot(inter[s * nb + k], recv[it][entry[s * nb + k]], preferred_element_type=jnp.float32)
-                ).astype(jnp.bfloat16)
-                for k in range(nb)
-            ]
+            zero = jnp.zeros((width, width), jnp.bfloat16)
+            scaled = []
+            for k in range(0, nb, 2):
+                own = jnp.concatenate([inter[s * nb + k], inter[s * nb + k + 1]], axis=1)
+                one = jnp.concatenate([recv[it][entry[s * nb + k]], zero], axis=1)
+                two = jnp.concatenate([zero, recv[it][entry[s * nb + k + 1]]], axis=1)
+                lifted = jnp.dot(own, jnp.concatenate([one, two], axis=0), preferred_element_type=jnp.float32)
+                scaled += [
+                    (coup[s, k] * lifted[:, :width]).astype(jnp.bfloat16),
+                    (coup[s, k + 1] * lifted[:, width:]).astype(jnp.bfloat16),
+                ]
             for k in range(0, nb, 2):
                 acc += lax.dot_general(
                     jnp.concatenate(scaled[k : k + 2], axis=1),

time: 76.9 us -> 76.9 us (level)
  no operation moved by 1% of the time
where the time goes in v8:
time: 76.9 us; the launch traced here: 76.8 us
  Pallas kernels  74.1 us (96%)
  other arithmetic  2.02 us (3%)
    pallas_call x1, Pallas kernels, body(): pl.pallas_call(kernel, out_shape=(jax.ShapeDtypeStruct(square, f32), jax....  74.1 us
    sub x1, other arithmetic, body(): return (last - residual / denom, residual)  2.02 us

profile of v8, /device:TPU:1, one launch (start us, length us, event | category | flops | bytes accessed | tf_op | source)
XLA Modules:
  0.0 76.8 jit_solution(7479400808127504716)
XLA Ops:
  0.6 74.1 %shard_map.104 = (f32[4,128,128]{2,1,0:T(8,128)}, f32[4,128,128]{2,1,0:T(8,128)}) custom-call(f32[4,16]{1,0:T(4,128)} %coup_hbm.1, s32[2,4]{1,0:T(2,128)} %bitcast.7, s32[1024]{0:T(1024)} %slot_hbm.1, f32[4,128,128]{2,1,0:T(8,128)} %amp_hbm.1, bf16[4,128,128]{2,1,0:T(8,128)(2,1)} %integ_hbm.1, f32[4,128]{1,0:T(4,128)} %ener_hbm.1, ...), custom_call_target="tpu_custom_call" | custom-call | tf_op jit(solution)/shard_map/pallas_call | solution.py:421
  74.8 2.0 %fusion.2 = (f32[4,128,128]{2,1,0:T(8,128)}, f32[4,128,128]{2,1,0:T(8,128)}) fusion(f32[4,128,128]{2,1,0:T(8,128)} %get-tuple-element.4, f32[4,128]{1,0:T(4,128)} %ener_hbm.1, f32[4,128,128]{2,1,0:T(8,128)} %get-tuple-element.5, bf16[4,128,128]{2,1,0:T(8,128)(2,1)} %integ_hbm.1), kind=kLoop, calls=%fused_computation.4 | loop fusion | flops 458752 | bytes 1181696 | tf_op jit(solution)/shard_map/sub | solution.py:447
